TPU v7x, 32 devices: a whole 2x2x4 slice. The times are simulated.
32 devices in a mesh: groups: 2 (over x), chan: 16 (over z, y, core).
Axes of the slice: x: 2, y: 2, z: 4, core: 2. Of those that a mesh axis runs over, the one named last changes fastest.
Arguments:
- samples: bfloat16 [2048, 2, 143, 256], P(('groups', 'chan')), parts along dimension 0, may hold values from -6 to 6
- flags: int32 [2048], P('groups'), parts along dimension 0, may hold values 0 or 1
- delays: int32 [256, 1024], replicated, may hold values from 0 to 255
- order: int32 [2048], P('groups'), parts along dimension 0, may hold values from 0 to 1023, each once
Outputs:
- visibilities: bfloat16 [512, 36, 2, 128, 128], P(('groups', 'chan')), parts along dimension 0
- beam_voltages: bfloat16 [512, 2, 113, 256], P(('groups', 'chan')), parts along dimension 0
There are 2 independent parts, one for each index of `groups`. A program takes and returns all parts, laid end to end along the dimension named above; an argument that names none is the same for every part. Nothing has to cross between parts.
Inputs may be any that keep to these rules, and one draw needn't show every extreme that they name: `order`: each antenna appears once.
All inputs are finite; a program needn't handle non-finite values.
Results may differ from a plain program's by a relative error of at most 0.008.
Values may be sent and summed in bfloat16 or wider, within the bound.
No kernel may reach another device: no remote copies, remote signals or barrier semaphores. Data moves between devices by JAX's collectives and lax.ppermute only.
A program may use at most 128 MiB of HBM per device.

v0:
```python
import math
import jax
import jax.numpy as jnp
import numpy as np
from jax import lax
from jax.sharding import PartitionSpec as P

ANTENNA_INPUTS = 1024
CHANNEL_COUNT = 256
VOLTAGE_BEAMS = 256
TAPS = 16
TILE_ANTENNAS = 128
WINDOW_SPECTRA = 128
OUTFRAMES = 113


def prototype(tap_count, chan_count):
    length = tap_count * chan_count
    counter = jnp.arange(length, dtype=jnp.float32)
    shifted = (counter - (length - 1) / 2.0) / chan_count
    window = 0.5 - 0.5 * jnp.cos(2.0 * math.pi * (counter + 0.5) / length)
    return (jnp.sinc(shifted) * window).reshape(tap_count, chan_count)


def dft_table(chan_count, direction):
    counter = jnp.arange(chan_count, dtype=jnp.int32)
    phase = counter[:, None] * counter[None, :] % chan_count
    angle = phase.astype(jnp.float32) * (2.0 * math.pi / chan_count)
    cosine = jnp.cos(angle)
    sine = jnp.sin(angle)
    top_rows = jnp.stack([cosine, -direction * sine], axis=1)
    bottom_rows = jnp.stack([direction * sine, cosine], axis=1)
    return jnp.stack([top_rows, bottom_rows], axis=0).astype(jnp.bfloat16)


def tile_pairs(tile_count):
    first_tiles = []
    second_tiles = []
    for row_tile in range(tile_count):
        for col_tile in range(row_tile, tile_count):
            first_tiles.append(row_tile)
            second_tiles.append(col_tile)
    return (np.array(first_tiles, np.int32), np.array(second_tiles, np.int32))


def per_device(samples, flags, delays, order):
    device_list = lax.axis_size("chan")
    local_channels = CHANNEL_COUNT // device_list
    local_antennas = samples.shape[0]
    filt = prototype(TAPS, CHANNEL_COUNT)
    filtered_frames = jnp.zeros((local_antennas, 2, WINDOW_SPECTRA, CHANNEL_COUNT), jnp.float32)
    for tap_step in range(TAPS):
        filtered_frames = (
            filtered_frames
            + filt[tap_step] * samples[:, :, tap_step : tap_step + WINDOW_SPECTRA, :]
        )
    filtered_frames = filtered_frames.astype(jnp.bfloat16)
    forward = dft_table(CHANNEL_COUNT, 1.0)
    channel_spectra = jnp.einsum(
        "arsj,rjuk->kaus", filtered_frames, forward, preferred_element_type=jnp.float32
    )
    channel_spectra = (channel_spectra * (1.0 / math.sqrt(CHANNEL_COUNT))).astype(jnp.bfloat16)
    channel_spectra = channel_spectra.reshape(
        device_list, local_channels, local_antennas, 2 * WINDOW_SPECTRA
    )
    flag_values = flags.astype(jnp.bfloat16)
    permuted_flags = jnp.take(flag_values, order, axis=0)
    tile_count = ANTENNA_INPUTS // TILE_ANTENNAS
    first_tiles, second_tiles = tile_pairs(tile_count)

    def correlate_channel(channel_rows):
        other = jnp.concatenate(
            [channel_rows[:, WINDOW_SPECTRA:], -channel_rows[:, :WINDOW_SPECTRA]], axis=1
        )
        stacked = jnp.stack([channel_rows, other], axis=0).reshape(
            2, tile_count, TILE_ANTENNAS, 2 * WINDOW_SPECTRA
        )
        picked = stacked[:, first_tiles]
        columns = channel_rows.reshape(tile_count, TILE_ANTENNAS, 2 * WINDOW_SPECTRA)[second_tiles]
        product = jnp.einsum("upis,pjs->puij", picked, columns, preferred_element_type=jnp.float32)
        return (product * (1.0 / WINDOW_SPECTRA)).astype(jnp.bfloat16)

    received = lax.all_to_all(channel_spectra, "chan", split_axis=0, concat_axis=2, tiled=True)
    turned_rows = received[0]
    permuted = jnp.take(turned_rows, order, axis=1) * permuted_flags[None, :, None]
    visibilities = lax.map(correlate_channel, permuted)
    masked = turned_rows * flag_values[None, :, None]
    other = jnp.concatenate([masked[:, :, WINDOW_SPECTRA:], -masked[:, :, :WINDOW_SPECTRA]], axis=2)
    stacked = jnp.concatenate([masked, other], axis=1)
    channel_ids = lax.axis_index("chan") * local_channels + jnp.arange(
        local_channels, dtype=jnp.int32
    )
    phase = delays[None, :, :] * channel_ids[:, None, None] % CHANNEL_COUNT
    angle = phase.astype(jnp.float32) * (2.0 * math.pi / CHANNEL_COUNT)
    weights = jnp.concatenate([jnp.cos(angle), jnp.sin(angle)], axis=2).astype(jnp.bfloat16)
    formed_beams = jnp.einsum("cba,cas->cbs", weights, stacked, preferred_element_type=jnp.float32)
    beams = (
        (formed_beams * (1.0 / math.sqrt(ANTENNA_INPUTS)))
        .astype(jnp.bfloat16)
        .reshape(local_channels, VOLTAGE_BEAMS, 2, WINDOW_SPECTRA)
    )
    inverse = dft_table(CHANNEL_COUNT, -1.0)
    arranged = lax.all_to_all(beams, "chan", split_axis=1, concat_axis=0, tiled=True)
    result = jnp.einsum("kbrs,rkuj->busj", arranged, inverse, preferred_element_type=jnp.float32)
    zeta = (result * (1.0 / math.sqrt(CHANNEL_COUNT))).astype(jnp.bfloat16)
    beam_local = zeta.shape[0]
    output = jnp.zeros((beam_local, 2, OUTFRAMES, CHANNEL_COUNT), jnp.float32)
    for tap_step in range(TAPS):
        output = output + filt[TAPS - 1 - tap_step] * zeta[:, :, tap_step : tap_step + OUTFRAMES, :]
    return (visibilities, output.astype(jnp.bfloat16))


def solution(mesh):
    in_specs = (P(("groups", "chan"), None, None, None), P("groups"), P(), P("groups"))
    out_specs = (
        P(("groups", "chan"), None, None, None, None),
        P(("groups", "chan"), None, None, None),
    )
    return jax.shard_map(
        per_device, mesh=mesh, in_specs=in_specs, out_specs=out_specs, check_vma=False
    )
```

profile of v0, /device:TPU:0, one launch (start us, length us, event | category | flops | bytes accessed | tf_op | source)
XLA Modules:
  0.0 672.2 jit_solution(12600181944661369911)
XLA Ops:
  3.7 115.9 %add_convert_fusion = bf16[64,2,128,256]{3,1,2,0:T(2,128)(2,1)S(1)} fusion(bf16[64,2,143,256]{3,1,2,0:T(2,128)(2,1)} %param.10, f32[256]{0:T(256)S(1)} %get-tuple-element.109, f32[256]{0:T(256)S(1)} %get-tuple-element.110, f32[256]{0:T(256)S(1)} %get-tuple-element.111, f32[256]{0:T(256)S(1)} %get-tuple-element.112, f32[256]{0:T(256)S(1)} %get-tuple-element.113, ...), kind=kLoop, calls=%fused_computation.37 | loop fusion | flops 201326592 | bytes 142622720 | tf_op jit(solution)/shard_map/convert_element_type | solution.py:57
  119.6 5.3 fusion.22
  124.9 20.5 %copy.30 = bf16[256,64,2,128]{3,2,1,0:T(2,128)(2,1)} copy(bf16[256,64,2,128]{3,0,1,2:T(8,128)(2,1)S(1)} %fusion.22) | data formatting | bytes 16777216 | tf_op jit(solution)/shard_map/convert_element_type | solution.py:62
  145.4 14.1 %reshape.195 = bf16[16,16,64,256]{3,2,1,0:T(8,128)(2,1)} reshape(bf16[256,64,2,128]{3,2,1,0:T(2,128)(2,1)} %copy.30) | data formatting | bytes 16777216 | tf_op jit(solution)/shard_map/reshape | solution.py:63
  159.6 7.6 %all-to-all-start = ((bf16[16,16,64,256]{3,2,1,0:T(8,128)(2,1)}), bf16[16,16,64,256]{3,2,1,0:T(8,128)(2,1)}, u32[]{:S(2)}, u32[]{:S(2)}) async-start(bf16[16,16,64,256]{3,2,1,0:T(8,128)(2,1)} %reshape.195), calls=%async_computation | async-start | bytes 16777216 | tf_op jit(solution)/shard_map/all_to_all | solution.py:83
  167.3 6.8 %gather_fusion.3 = bf16[1024]{0:T(1024)(128)(2,1)S(1)} fusion(bf16[1024]{0:T(1024)(128)(2,1)S(1)} %convert_element_type.187, s32[1024]{0:T(1024)S(1)} %fusion.81), kind=kCustom, calls=%fused_computation.3 | custom fusion | bytes 8192 | tf_op jit(solution)/shard_map/jit(_take)/gather | solution.py:67
  174.1 69.0 %cosine_convert_fusion = (bf16[16,256,1024]{2,1,0:T(8,128)(2,1)}, bf16[16,256,1024]{2,1,0:T(8,128)(2,1)}) fusion(s32[16]{0:T(128)S(1)} %iota_add_fusion.2, s32[256,1024]{1,0:T(8,128)S(1)} %copy-done), kind=kLoop, calls=%fused_computation.36 | loop fusion | flops 67108864 | bytes 17825856 | tf_op jit(solution)/shard_map/convert
  243.1 74.7 %all-to-all-done = bf16[16,16,64,256]{3,2,1,0:T(8,128)(2,1)} async-done(((bf16[16,16,64,256]{3,2,1,0:T(8,128)(2,1)}), bf16[16,16,64,256]{3,2,1,0:T(8,128)(2,1)}, u32[]{:S(2)}, u32[]{:S(2)}) %all-to-all-start) | async-done | bytes 8388640 | tf_op jit(solution)/shard_map/all_to_all | solution.py:83
  317.8 8.3 %copy.31 = bf16[1,16,16,64,256]{4,3,2,1,0:T(8,128)(2,1)} copy(bf16[1,16,16,64,256]{4,3,1,2,0:T(8,128)(2,1)} %bitcast.10) | data formatting | bytes 16777216 | tf_op jit(solution)/shard_map/all_to_all | solution.py:83
  326.0 12.3 %copy.34 = bf16[16,1024,256]{1,2,0:T(8,128)(2,1)} copy(bf16[16,1024,256]{2,1,0:T(8,128)(2,1)} %bitcast.95) | data formatting | bytes 16777216 | tf_op jit(solution)/shard_map/squeeze | solution.py:84
  338.3 11.4 %copy.32 = bf16[16,1024,256]{2,0,1:T(8,128)(2,1)} copy(bf16[16,1024,256]{2,1,0:T(8,128)(2,1)} %bitcast.96) | data formatting | bytes 16777216 | tf_op jit(solution)/shard_map/squeeze | solution.py:84
  349.7 7.1 %broadcast_multiply_fusion = bf16[16,1024,256]{1,2,0:T(8,128)(2,1)} fusion(bf16[16,1024,256]{1,2,0:T(8,128)(2,1)} %copy.34, bf16[1024]{0:T(1024)(128)(2,1)S(1)} %convert_element_type.187), kind=kLoop, calls=%fused_computation.47 | loop fusion | flops 4194304 | bytes 16779264 | tf_op jit(solution)/shard_map/mul | solution.py:87
  356.9 5.1 fusion.85
  361.9 11.3 %multiply_convert_fusion.1 = bf16[16,256,256]{1,2,0:T(8,128)(2,1)S(1)} fusion(bf16[16,1024,128]{1,2,0:T(8,128)(2,1)} %get-tuple-element.99, bf16[16,1024,128]{1,2,0:T(8,128)(2,1)S(1)} %get-tuple-element.98, bf16[16,1024,256]{1,2,0:T(8,128)(2,1)} %broadcast_multiply_fusion, bf16[16,256,1024]{2,1,0:T(8,128)(2,1)} %get-tuple-element.101, ...), kind=kOutput, calls=%fused_computation.46 | convolution fusion | flops 4380950528 | bytes 35651584 | tf_op jit(solution)/shard_map/cba,cas->cbs/dot_general | solution.py:96
  377.3 36.5 %all-to-all-start.1 = ((bf16[16,256,2,128]{3,2,0,1:T(2,128)(2,1)}), bf16[16,256,2,128]{3,2,0,1:T(2,128)(2,1)}, u32[]{:S(2)}, u32[]{:S(2)}) async-start(bf16[16,256,2,128]{3,2,0,1:T(2,128)(2,1)} %copy.35), calls=%async_computation.1 | async-start | bytes 4194304 | tf_op jit(solution)/shard_map/all_to_all | solution.py:103
  413.9 13.1 %gather_fusion.2 = bf16[1024,16,256]{2,1,0:T(8,128)(2,1)} fusion(bf16[16,1024,256]{2,0,1:T(8,128)(2,1)} %copy.32, s32[1024]{0:T(1024)S(1)} %fusion.81), kind=kCustom, calls=%fused_computation.2 | custom fusion | bytes 16781312 | tf_op jit(solution)/shard_map/jit(_take)/gather | solution.py:85
  427.0 10.1 %multiply_bitcast_fusion = bf16[16,1024,256]{2,0,1:T(8,128)(2,1)} fusion(bf16[1024,16,256]{2,1,0:T(8,128)(2,1)} %gather_fusion.2, pred[1024]{0:T(1024)(128)(4,1)S(1)} %get-tuple-element.95, bf16[1024]{0:T(1024)(128)(2,1)S(1)} %get-tuple-element.94), kind=kLoop, calls=%fused_computation.42 | loop fusion | flops 8388608 | bytes 16780288 | tf_op jit(solution)/shard_map/mul | solution.py:85
  437.1 9.7 %copy.33 = bf16[16,1024,256]{2,1,0:T(8,128)(2,1)} copy(bf16[16,1024,256]{2,0,1:T(8,128)(2,1)} %multiply_bitcast_fusion) | data formatting | bytes 16777216
  446.8 205.1 %while.12 = (s32[]{:T(128)}, bf16[16,36,2,128,128]{4,3,2,1,0:T(8,128)(2,1)}, bf16[16,1024,256]{2,1,0:T(8,128)(2,1)}, s32[]{:T(128)}, s32[36]{0:T(128)S(1)}, /*index=5*/s32[36]{0:T(128)S(1)}) while((s32[]{:T(128)}, bf16[16,36,2,128,128]{4,3,2,1,0:T(8,128)(2,1)}, bf16[16,1024,256]{2,1,0:T(8,128)(2,1)}, s32[]{:T(128)}, ...), condition=%wide.region_1.2_spmd.clone.clone, body=%wide.region_0.1_spmd.sunk.clone.clone.sunk | while | flops 608045056 | bytes 29893772 | solution.py:86
  449.2 4.5 gather_fusion.1
  454.4 5.1 fusion.97
  462.0 4.5 gather_fusion.1
  467.3 5.1 fusion.97
  474.8 4.5 gather_fusion.1
  480.1 5.1 fusion.97
  487.7 4.5 gather_fusion.1
  492.9 5.1 fusion.97
  500.5 4.5 gather_fusion.1
  505.7 5.1 fusion.97
  513.3 4.5 gather_fusion.1
  518.5 5.1 fusion.97
  526.1 4.5 gather_fusion.1
  531.4 5.1 fusion.97
  538.9 4.5 gather_fusion.1
  544.2 5.1 fusion.97
  551.7 4.5 gather_fusion.1
  557.0 5.1 fusion.97
  564.6 4.5 gather_fusion.1
  569.8 5.1 fusion.97
  577.4 4.5 gather_fusion.1
  582.6 5.1 fusion.97
  595.4 5.1 fusion.97
  608.3 5.1 fusion.97
  621.1 5.1 fusion.97
  633.9 5.1 fusion.97
  641.5 4.5 gather_fusion.1
  646.7 5.1 fusion.97
  660.5 8.5 %add_convert_fusion.1 = bf16[16,2,113,256]{3,2,0,1:T(8,128)(2,1)S(1)} fusion(bf16[16,2,128,256]{3,2,0,1:T(8,128)(2,1)S(1)} %fusion.34, f32[256]{0:T(256)S(1)} %get-tuple-element.108, f32[256]{0:T(256)S(1)} %get-tuple-element.123, f32[256]{0:T(256)S(1)} %get-tuple-element.122, f32[256]{0:T(256)S(1)} %get-tuple-element.121, f32[256]{0:T(256)S(1)} %get-tuple-element.120, ...), kind=kLoop, calls=%fused_computation.48 | loop fusion | flops 44433408 | bytes 31490048 | tf_op jit(solution)/shard_map/convert_element_type | solution.py:110
  (163 shorter events, 86.7 us)
Async XLA Ops:
  159.6 7.6 %copy-start.6 = (s32[1024]{0:T(1024)S(1)}, s32[1024]{0:T(1024)}, u32[]{:S(2)}) copy-start(s32[1024]{0:T(1024)} %param.11) | copy-start | bytes 12292
  159.6 7.7 %copy-start.3 = (s32[1024]{0:T(1024)S(1)}, s32[1024]{0:T(1024)}, u32[]{:S(2)}) copy-start(s32[1024]{0:T(1024)} %param.13) | copy-start | bytes 12292
  159.6 14.5 %copy-start = (s32[256,1024]{1,0:T(8,128)S(1)}, s32[256,1024]{1,0:T(8,128)}, u32[]{:S(2)}) copy-start(s32[256,1024]{1,0:T(8,128)} %param.12) | copy-start | bytes 3145732
  159.6 158.2 %all-to-all-start = ((bf16[16,16,64,256]{3,2,1,0:T(8,128)(2,1)}), bf16[16,16,64,256]{3,2,1,0:T(8,128)(2,1)}, u32[]{:S(2)}, u32[]{:S(2)}) async-start(bf16[16,16,64,256]{3,2,1,0:T(8,128)(2,1)} %reshape.195), calls=%async_computation | async-start | bytes 16777216 | tf_op jit(solution)/shard_map/all_to_all | solution.py:83
  377.3 274.5 %all-to-all-start.1 = ((bf16[16,256,2,128]{3,2,0,1:T(2,128)(2,1)}), bf16[16,256,2,128]{3,2,0,1:T(2,128)(2,1)}, u32[]{:S(2)}, u32[]{:S(2)}) async-start(bf16[16,256,2,128]{3,2,0,1:T(2,128)(2,1)} %copy.35), calls=%async_computation.1 | async-start | bytes 4194304 | tf_op jit(solution)/shard_map/all_to_all | solution.py:103
  437.1 9.7 %copy-start.4 = (s32[36]{0:T(128)S(1)}, s32[36]{0:T(128)}, u32[]{:S(2)}) copy-start(s32[36]{0:T(128)} %constant.301) | copy-start | bytes 436
  437.1 9.7 %copy-start.5 = (s32[36]{0:T(128)S(1)}, s32[36]{0:T(128)}, u32[]{:S(2)}) copy-start(s32[36]{0:T(128)} %constant.302) | copy-start | bytes 436
  651.8 5.8 copy-start.1
  651.8 5.8 copy-start.2
where the time goes:
time: 675 us; the launch traced here: 672 us
  local copies, waits for them, and re-layouts  227 us (34%)
  other arithmetic  223 us (33%)
  matrix products  102 us (15%)
  waiting for transfers between devices  74.7 us (11%)
  starting transfers between devices  44.2 us (7%)
    convert_element_type x1, other arithmetic, per_device(): filtered_frames = filtered_frames.astype(jnp.bfloat16)  116 us
    dot_general x16, matrix products, correlate_channel(): jnp.einsum('upis,pjs->puij', picked, columns, preferred_element_type=jnp....  82.3 us
    all_to_all x1, waiting for transfers between devices, per_device(): lax.all_to_all(channel_spectra, 'chan', split_axis=0, concat_axis=2, tile...  74.7 us
    gather x16, local copies, waits for them, and re-layouts, correlate_channel(): picked = stacked[:, first_tiles]  72.6 us
    another operation x3, other arithmetic  71.1 us
    all_to_all x1, starting transfers between devices, per_device(): lax.all_to_all(beams, 'chan', split_axis=1, concat_axis=0, tiled=True)  36.5 us
    squeeze x2, local copies, waits for them, and re-layouts, per_device(): turned_rows = received[0]  23.7 us
    convert_element_type x1, local copies, waits for them, and re-layouts, per_device(): (channel_spectra * (1.0 / math.sqrt(CHANNEL_COUNT))).astype(jnp.bfloat16)  20.5 us
  transfers between devices with their start and end apart: 2, of which 1 were waited for; matrix products, arithmetic and copies ran while one was open for 47% of the time, Pallas kernels for 0%

commit v1 on v0

--- a/solution.py
+++ b/solution.py
@@ -100,7 +100,10 @@
         .reshape(local_channels, VOLTAGE_BEAMS, 2, WINDOW_SPECTRA)
     )
     inverse = dft_table(CHANNEL_COUNT, -1.0)
-    arranged = lax.all_to_all(beams, "chan", split_axis=1, concat_axis=0, tiled=True)
+    arranged = jnp.concatenate(
+        lax.all_to_all(jnp.stack(jnp.split(beams, lax.axis_size("chan"), axis=1)), "chan", 0, 0),
+        axis=0,
+    )
     result = jnp.einsum("kbrs,rkuj->busj", arranged, inverse, preferred_element_type=jnp.float32)
     zeta = (result * (1.0 / math.sqrt(CHANNEL_COUNT))).astype(jnp.bfloat16)
     beam_local = zeta.shape[0]

time: 675 us -> 729 us (1.080)
  local copies, waits for them, and re-layouts: 227 us -> 275 us
    unnamed x16 -> x113, local copies, waits for them, and re-layouts: 12.8 us -> 58.7 us
    split x0 -> x1, local copies, waits for them, and re-layouts: none -> 7.38 us  [per_device(): jnp.split(beams, lax.axis_size('chan'), axis=1)]
  transfers between devices with their start and end apart: 2 -> 2, of which waited for: 1 -> 1; matrix products, arithmetic and copies ran while one was open for 47% -> 44% of each run, Pallas kernels for 0% -> 0%
where the time goes in v1:
time: 729 us; the launch traced here: 719 us
  local copies, waits for them, and re-layouts  275 us (38%)
  other arithmetic  223 us (31%)
  matrix products  100 us (14%)
  waiting for transfers between devices  74.7 us (10%)
  starting transfers between devices  44.8 us (6%)
    convert_element_type x1, other arithmetic, per_device(): filtered_frames = filtered_frames.astype(jnp.bfloat16)  116 us
    dot_general x16, matrix products, correlate_channel(): jnp.einsum('upis,pjs->puij', picked, columns, preferred_element_type=jnp....  82.2 us
    all_to_all x1, waiting for transfers between devices, per_device(): lax.all_to_all(channel_spectra, 'chan', split_axis=0, concat_axis=2, tile...  74.7 us
    gather x16, local copies, waits for them, and re-layouts, correlate_channel(): picked = stacked[:, first_tiles]  73.1 us
    another operation x3, other arithmetic  71.1 us
    unnamed x113, local copies, waits for them, and re-layouts  58.7 us
    all_to_all x1, starting transfers between devices, per_device(): lax.all_to_all(jnp.stack(jnp.split(beams, lax.axis_size('chan'), axis=1))...  36.8 us
    squeeze x2, local copies, waits for them, and re-layouts, per_device(): turned_rows = received[0]  23.7 us
  transfers between devices with their start and end apart: 2, of which 1 were waited for; matrix products, arithmetic and copies ran while one was open for 44% of the time, Pallas kernels for 0%

profile of v1, /device:TPU:0, one launch (start us, length us, event | category | flops | bytes accessed | tf_op | source)
XLA Modules:
  0.0 719.4 jit_solution(10455626057562478742)
XLA Ops:
  3.9 115.9 %add_convert_fusion = bf16[64,2,128,256]{3,1,2,0:T(2,128)(2,1)S(1)} fusion(bf16[64,2,143,256]{3,1,2,0:T(2,128)(2,1)} %param.10, f32[256]{0:T(256)S(1)} %get-tuple-element.120, f32[256]{0:T(256)S(1)} %get-tuple-element.121, f32[256]{0:T(256)S(1)} %get-tuple-element.122, f32[256]{0:T(256)S(1)} %get-tuple-element.123, f32[256]{0:T(256)S(1)} %get-tuple-element.124, ...), kind=kLoop, calls=%fused_computation.37 | loop fusion | flops 201326592 | bytes 142622720 | tf_op jit(solution)/shard_map/convert_element_type | solution.py:57
  119.9 5.3 fusion.22
  125.2 20.5 %copy.18 = bf16[256,64,2,128]{3,2,1,0:T(2,128)(2,1)} copy(bf16[256,64,2,128]{3,0,1,2:T(8,128)(2,1)S(1)} %fusion.22) | data formatting | bytes 16777216 | tf_op jit(solution)/shard_map/convert_element_type | solution.py:62
  145.8 14.0 %reshape.198 = bf16[16,16,64,256]{3,2,1,0:T(8,128)(2,1)} reshape(bf16[256,64,2,128]{3,2,1,0:T(2,128)(2,1)} %copy.18) | data formatting | bytes 16777216 | tf_op jit(solution)/shard_map/reshape | solution.py:63
  159.8 8.1 %all-to-all-start = ((bf16[16,16,64,256]{3,2,1,0:T(8,128)(2,1)}), bf16[16,16,64,256]{3,2,1,0:T(8,128)(2,1)}, u32[]{:S(2)}, u32[]{:S(2)}) async-start(bf16[16,16,64,256]{3,2,1,0:T(8,128)(2,1)} %reshape.198), calls=%async_computation | async-start | bytes 16777216 | tf_op jit(solution)/shard_map/all_to_all | solution.py:83
  168.0 6.8 gather_fusion.3
  174.8 69.0 %cosine_convert_fusion = (bf16[16,256,1024]{2,1,0:T(8,128)(2,1)}, bf16[16,256,1024]{2,1,0:T(8,128)(2,1)}) fusion(s32[16]{0:T(128)S(1)} %iota_add_fusion.2, s32[256,1024]{1,0:T(8,128)S(1)} %copy-done), kind=kLoop, calls=%fused_computation.36 | loop fusion | flops 67108864 | bytes 17825856 | tf_op jit(solution)/shard_map/convert
  243.8 74.7 %all-to-all-done = bf16[16,16,64,256]{3,2,1,0:T(8,128)(2,1)} async-done(((bf16[16,16,64,256]{3,2,1,0:T(8,128)(2,1)}), bf16[16,16,64,256]{3,2,1,0:T(8,128)(2,1)}, u32[]{:S(2)}, u32[]{:S(2)}) %all-to-all-start) | async-done | bytes 8388640 | tf_op jit(solution)/shard_map/all_to_all | solution.py:83
  318.4 8.3 %copy.19 = bf16[1,16,16,64,256]{4,3,2,1,0:T(8,128)(2,1)} copy(bf16[1,16,16,64,256]{4,3,1,2,0:T(8,128)(2,1)} %bitcast.10) | data formatting | bytes 16777216 | tf_op jit(solution)/shard_map/all_to_all | solution.py:83
  326.8 12.3 %copy.22 = bf16[16,1024,256]{1,2,0:T(8,128)(2,1)} copy(bf16[16,1024,256]{2,1,0:T(8,128)(2,1)} %bitcast.125) | data formatting | bytes 16777216 | tf_op jit(solution)/shard_map/squeeze | solution.py:84
  339.0 11.4 %copy.20 = bf16[16,1024,256]{2,0,1:T(8,128)(2,1)} copy(bf16[16,1024,256]{2,1,0:T(8,128)(2,1)} %bitcast.126) | data formatting | bytes 16777216 | tf_op jit(solution)/shard_map/squeeze | solution.py:84
  350.5 7.2 broadcast_multiply_fusion
  357.7 5.3 fusion.85
  363.0 11.2 %multiply_convert_fusion.1 = bf16[16,256,256]{1,2,0:T(8,128)(2,1)S(1)} fusion(bf16[16,1024,128]{1,2,0:T(8,128)(2,1)} %get-tuple-element.94, bf16[16,1024,128]{1,2,0:T(8,128)(2,1)S(1)} %get-tuple-element.93, bf16[16,1024,256]{1,2,0:T(8,128)(2,1)} %broadcast_multiply_fusion, bf16[16,256,1024]{2,1,0:T(8,128)(2,1)} %get-tuple-element.112, ...), kind=kOutput, calls=%fused_computation.46 | convolution fusion | flops 4380950528 | bytes 35651584 | tf_op jit(solution)/shard_map/cba,cas->cbs/dot_general | solution.py:96
  374.2 7.4 %fusion.86 = (bf16[16,16,2,128]{1,3,2,0:T(8,128)(2,1)S(1)}, bf16[16,16,2,128]{1,3,2,0:T(8,128)(2,1)S(1)}, bf16[16,16,2,128]{1,3,2,0:T(8,128)(2,1)S(1)}, bf16[16,...) fusion(bf16[16,256,2,128]{1,3,2,0:T(8,128)(2,1)S(1)} %bitcast.124), kind=kLoop, calls=%fused_computation.139 | loop fusion | bytes 4194304 | tf_op jit(solution)/shard_map/split | solution.py:104
  427.9 36.8 %all-to-all-start.1 = ((bf16[16,16,16,2,128]{4,2,3,1,0:T(8,128)(2,1)}), bf16[16,16,16,2,128]{4,2,3,1,0:T(8,128)(2,1)}, u32[]{:S(2)}, u32[]{:S(2)}) async-start(bf16[16,16,16,2,128]{4,2,3,1,0:T(8,128)(2,1)} %bitcast_dynamic-update-slice_fusion), calls=%async_computation.1 | async-start | bytes 4194304 | tf_op jit(solution)/shard_map/all_to_all | solution.py:104
  464.7 12.9 %gather_fusion.2 = bf16[1024,16,256]{2,1,0:T(8,128)(2,1)} fusion(bf16[16,1024,256]{2,0,1:T(8,128)(2,1)} %copy.20, s32[1024]{0:T(1024)S(1)} %fusion.81), kind=kCustom, calls=%fused_computation.2 | custom fusion | bytes 16781312 | tf_op jit(solution)/shard_map/jit(_take)/gather | solution.py:85
  477.6 10.1 %multiply_bitcast_fusion = bf16[16,1024,256]{2,0,1:T(8,128)(2,1)} fusion(bf16[1024,16,256]{2,1,0:T(8,128)(2,1)} %gather_fusion.2, pred[1024]{0:T(1024)(128)(4,1)S(1)} %get-tuple-element.90, bf16[1024]{0:T(1024)(128)(2,1)S(1)} %get-tuple-element.89), kind=kLoop, calls=%fused_computation.42 | loop fusion | flops 8388608 | bytes 16780288 | tf_op jit(solution)/shard_map/mul | solution.py:85
  487.7 9.7 %copy.21 = bf16[16,1024,256]{2,1,0:T(8,128)(2,1)} copy(bf16[16,1024,256]{2,0,1:T(8,128)(2,1)} %multiply_bitcast_fusion) | data formatting | bytes 16777216
  497.5 205.7 %while.12 = (s32[]{:T(128)}, bf16[16,36,2,128,128]{4,3,2,1,0:T(8,128)(2,1)}, bf16[16,1024,256]{2,1,0:T(8,128)(2,1)}, s32[]{:T(128)}, s32[36]{0:T(128)S(1)}, /*index=5*/s32[36]{0:T(128)S(1)}) while((s32[]{:T(128)}, bf16[16,36,2,128,128]{4,3,2,1,0:T(8,128)(2,1)}, bf16[16,1024,256]{2,1,0:T(8,128)(2,1)}, s32[]{:T(128)}, ...), condition=%wide.region_1.2_spmd.clone.clone, body=%wide.region_0.1_spmd.sunk.clone.clone.sunk | while | flops 608045056 | bytes 29893772 | solution.py:86
  500.0 4.6 gather_fusion.1
  505.2 5.1 fusion.98
  518.1 5.1 fusion.98
  525.7 4.6 gather_fusion.1
  531.0 5.1 fusion.98
  543.8 5.1 fusion.98
  551.4 4.6 gather_fusion.1
  556.7 5.1 fusion.98
  564.2 4.6 gather_fusion.1
  569.5 5.1 fusion.98
  582.4 5.1 fusion.98
  589.9 4.6 gather_fusion.1
  595.2 5.1 fusion.98
  602.8 4.6 gather_fusion.1
  608.1 5.1 fusion.98
  620.9 5.1 fusion.98
  628.5 4.6 gather_fusion.1
  633.8 5.1 fusion.98
  641.3 4.6 gather_fusion.1
  646.6 5.1 fusion.98
  659.5 5.1 fusion.98
  667.0 4.6 gather_fusion.1
  672.3 5.1 fusion.98
  679.9 4.6 gather_fusion.1
  685.2 5.1 fusion.98
  692.7 4.6 gather_fusion.1
  698.0 5.1 fusion.98
  707.8 8.2 %add_convert_fusion.1 = bf16[16,2,113,256]{3,2,0,1:T(8,128)(2,1)S(1)} fusion(bf16[16,2,128,256]{3,2,0,1:T(8,128)(2,1)S(1)} %fusion.34, f32[256]{0:T(256)S(1)} %copy-done.8, f32[256]{0:T(256)S(1)} %copy-done.38, f32[256]{0:T(256)S(1)} %copy-done.36, f32[256]{0:T(256)S(1)} %copy-done.34, f32[256]{0:T(256)S(1)} %copy-done.32, f32[256]{0:T(256)S(1)} %copy-done.30, ...), kind=kLoop, calls=%fused_computation.48 | loop fusion | flops 44433408 | bytes 31490048 | tf_op jit(solution)/shard_map/convert_element_type | solution.py:113
  (259 shorter events, 129.4 us)
Async XLA Ops:
  2.8 116.9 %copy-start.7 = (f32[256]{0:T(256)}, f32[256]{0:T(256)S(1)}, u32[]{:S(2)}) copy-start(f32[256]{0:T(256)S(1)} %get-tuple-element.119) | copy-start | bytes 3076
  2.9 116.9 %copy-start.9 = (f32[256]{0:T(256)}, f32[256]{0:T(256)S(1)}, u32[]{:S(2)}) copy-start(f32[256]{0:T(256)S(1)} %get-tuple-element.120) | copy-start | bytes 3076
  2.9 116.9 %copy-start.11 = (f32[256]{0:T(256)}, f32[256]{0:T(256)S(1)}, u32[]{:S(2)}) copy-start(f32[256]{0:T(256)S(1)} %get-tuple-element.121) | copy-start | bytes 3076
  2.9 116.9 %copy-start.13 = (f32[256]{0:T(256)}, f32[256]{0:T(256)S(1)}, u32[]{:S(2)}) copy-start(f32[256]{0:T(256)S(1)} %get-tuple-element.122) | copy-start | bytes 3076
  2.9 116.9 %copy-start.15 = (f32[256]{0:T(256)}, f32[256]{0:T(256)S(1)}, u32[]{:S(2)}) copy-start(f32[256]{0:T(256)S(1)} %get-tuple-element.123) | copy-start | bytes 3076
  2.9 116.9 %copy-start.17 = (f32[256]{0:T(256)}, f32[256]{0:T(256)S(1)}, u32[]{:S(2)}) copy-start(f32[256]{0:T(256)S(1)} %get-tuple-element.124) | copy-start | bytes 3076
  2.9 116.9 %copy-start.19 = (f32[256]{0:T(256)}, f32[256]{0:T(256)S(1)}, u32[]{:S(2)}) copy-start(f32[256]{0:T(256)S(1)} %get-tuple-element.125) | copy-start | bytes 3076
  2.9 116.9 %copy-start.21 = (f32[256]{0:T(256)}, f32[256]{0:T(256)S(1)}, u32[]{:S(2)}) copy-start(f32[256]{0:T(256)S(1)} %get-tuple-element.126) | copy-start | bytes 3076
  2.9 116.9 %copy-start.23 = (f32[256]{0:T(256)}, f32[256]{0:T(256)S(1)}, u32[]{:S(2)}) copy-start(f32[256]{0:T(256)S(1)} %get-tuple-element.127) | copy-start | bytes 3076
  2.9 116.9 %copy-start.25 = (f32[256]{0:T(256)}, f32[256]{0:T(256)S(1)}, u32[]{:S(2)}) copy-start(f32[256]{0:T(256)S(1)} %get-tuple-element.128) | copy-start | bytes 3076
  2.9 116.9 %copy-start.27 = (f32[256]{0:T(256)}, f32[256]{0:T(256)S(1)}, u32[]{:S(2)}) copy-start(f32[256]{0:T(256)S(1)} %get-tuple-element.129) | copy-start | bytes 3076
  3.0 116.9 %copy-start.29 = (f32[256]{0:T(256)}, f32[256]{0:T(256)S(1)}, u32[]{:S(2)}) copy-start(f32[256]{0:T(256)S(1)} %get-tuple-element.130) | copy-start | bytes 3076
  3.0 116.9 %copy-start.31 = (f32[256]{0:T(256)}, f32[256]{0:T(256)S(1)}, u32[]{:S(2)}) copy-start(f32[256]{0:T(256)S(1)} %get-tuple-element.131) | copy-start | bytes 3076
  3.0 116.9 %copy-start.33 = (f32[256]{0:T(256)}, f32[256]{0:T(256)S(1)}, u32[]{:S(2)}) copy-start(f32[256]{0:T(256)S(1)} %get-tuple-element.132) | copy-start | bytes 3076
  3.0 116.9 %copy-start.35 = (f32[256]{0:T(256)}, f32[256]{0:T(256)S(1)}, u32[]{:S(2)}) copy-start(f32[256]{0:T(256)S(1)} %get-tuple-element.133) | copy-start | bytes 3076
  3.0 116.9 %copy-start.37 = (f32[256]{0:T(256)}, f32[256]{0:T(256)S(1)}, u32[]{:S(2)}) copy-start(f32[256]{0:T(256)S(1)} %get-tuple-element.134) | copy-start | bytes 3076
  159.8 8.1 %copy-start.39 = (s32[1024]{0:T(1024)S(1)}, s32[1024]{0:T(1024)}, u32[]{:S(2)}) copy-start(s32[1024]{0:T(1024)} %param.11) | copy-start | bytes 12292
  159.8 8.1 %copy-start.4 = (s32[1024]{0:T(1024)S(1)}, s32[1024]{0:T(1024)}, u32[]{:S(2)}) copy-start(s32[1024]{0:T(1024)} %param.13) | copy-start | bytes 12292
  159.8 15.0 %copy-start = (s32[256,1024]{1,0:T(8,128)S(1)}, s32[256,1024]{1,0:T(8,128)}, u32[]{:S(2)}) copy-start(s32[256,1024]{1,0:T(8,128)} %param.12) | copy-start | bytes 3145732
  159.8 158.6 %all-to-all-start = ((bf16[16,16,64,256]{3,2,1,0:T(8,128)(2,1)}), bf16[16,16,64,256]{3,2,1,0:T(8,128)(2,1)}, u32[]{:S(2)}, u32[]{:S(2)}) async-start(bf16[16,16,64,256]{3,2,1,0:T(8,128)(2,1)} %reshape.198), calls=%async_computation | async-start | bytes 16777216 | tf_op jit(solution)/shard_map/all_to_all | solution.py:83
  409.2 14.8 %copy-start.1 = (bf16[16,16,2,128]{3,1,2,0:T(8,128)(2,1)S(1)}, bf16[16,16,2,128]{3,1,2,0:T(8,128)(2,1)}, u32[]{:S(2)}) copy-start(bf16[16,16,2,128]{3,1,2,0:T(8,128)(2,1)} %copy.59) | copy-start | bytes 393220
  427.9 275.3 %all-to-all-start.1 = ((bf16[16,16,16,2,128]{4,2,3,1,0:T(8,128)(2,1)}), bf16[16,16,16,2,128]{4,2,3,1,0:T(8,128)(2,1)}, u32[]{:S(2)}, u32[]{:S(2)}) async-start(bf16[16,16,16,2,128]{4,2,3,1,0:T(8,128)(2,1)} %bitcast_dynamic-update-slice_fusion), calls=%async_computation.1 | async-start | bytes 4194304 | tf_op jit(solution)/shard_map/all_to_all | solution.py:104
  487.7 9.7 %copy-start.5 = (s32[36]{0:T(128)S(1)}, s32[36]{0:T(128)}, u32[]{:S(2)}) copy-start(s32[36]{0:T(128)} %constant.348) | copy-start | bytes 436
  487.7 9.7 %copy-start.6 = (s32[36]{0:T(128)S(1)}, s32[36]{0:T(128)}, u32[]{:S(2)}) copy-start(s32[36]{0:T(128)} %constant.349) | copy-start | bytes 436
  497.5 208.9 %copy-start.2 = (bf16[1,256,2,256]{1,3,2,0:T(8,128)(2,1)S(1)}, bf16[1,256,2,256]{1,3,2,0:T(8,128)(2,1)}, u32[]{:S(2)}) copy-start(bf16[1,256,2,256]{1,3,2,0:T(8,128)(2,1)} %get-tuple-element.113) | copy-start | bytes 786436
  497.5 208.9 %copy-start.3 = (bf16[1,256,2,256]{1,3,2,0:T(8,128)(2,1)S(1)}, bf16[1,256,2,256]{1,3,2,0:T(8,128)(2,1)}, u32[]{:S(2)}) copy-start(bf16[1,256,2,256]{1,3,2,0:T(8,128)(2,1)} %get-tuple-element.118) | copy-start | bytes 786436
  706.2 1.5 copy-start.8
  706.2 1.5 copy-start.10
  706.2 1.5 copy-start.12
  706.2 1.5 copy-start.14
  706.2 1.5 copy-start.16
  706.2 1.5 copy-start.18
  706.2 1.5 copy-start.20
  706.2 1.5 copy-start.22
  706.2 1.5 copy-start.24
  706.2 1.5 copy-start.26
  706.3 1.5 copy-start.28
  706.3 1.5 copy-start.30
  706.3 1.5 copy-start.32
  706.3 1.5 copy-start.34
  706.3 1.5 copy-start.36
  706.3 1.5 copy-start.38
